TPU v7x, 512 devices: a whole 4x8x8 slice. The times are simulated.
512 devices in a mesh: section: 16 (over z_lo, x), seq: 32 (over z_hi, y, core).
Axes of the slice: x: 4, y: 8, z: 8 (z_hi: 2, z_lo: 4; z = z_hi * 4 + z_lo), core: 2. Of those that a mesh axis runs over, the one named last changes fastest.
Arguments:
- features: bfloat16 [16, 4096, 4096], P('section', 'seq'), may hold values from -6 to 6
- queries: bfloat16 [16, 4096, 4096], P('section', 'seq'), may hold values from -52 to 52
- out_grad: bfloat16 [16, 4096, 4096], P('section', 'seq'), may hold values from -0.09375 to 0.09375
- doc_ids: int32 [16, 4096], P('section', 'seq'), may hold values from 0 to 15, never falling along the last dimension, each value on 1 to 512 neighbouring positions
- key_weight: bfloat16 [4096, 512], P('section'), may hold values from -0.09375 to 0.09375
Outputs:
- value_weight_grad: float32 [4096, 512], P('seq', 'section')
All inputs are finite; a program needn't handle non-finite values.
Results may differ from a plain program's by a relative error of at most 0.012.
Values may be sent and summed in bfloat16 or wider, within the bound.
No kernel may reach another device: no remote copies, remote signals or barrier semaphores. Data moves between devices by JAX's collectives and lax.ppermute only.
A program may use at most 64 MiB of HBM per device.

v0:
```python
import math

import jax
import jax.numpy as jnp
from jax import lax
from jax.sharding import Mesh
from jax.sharding import PartitionSpec as P

HQ = 32
KVH = 4
HD = 128
REACH = 4
SECTION = ("section_0", "section_1")
SEQ = ("seq_0", "seq_1", "seq_2")


def in_order(blocks, dim):
    shape = list(blocks.shape[1:])
    shape[dim] *= blocks.shape[0]
    return jnp.moveaxis(blocks, 0, dim).reshape(shape)


def stacked_from(x, axes, order):
    blocks = x
    for k in order:
        blocks = lax.all_gather(blocks, axes[k])
    done = order[::-1]
    back = [done.index(k) for k in range(len(axes))]
    blocks = blocks.transpose(*back, *range(len(axes), blocks.ndim))
    return blocks.reshape(-1, *x.shape)


def gather_axes(x, axes, order, dim):
    return in_order(stacked_from(x, axes, order), dim)


def copy_for_each(x, axis):
    copies = jnp.broadcast_to(x, (lax.axis_size(axis), *x.shape))
    return lax.all_to_all(copies, axis, split_axis=0, concat_axis=0, tiled=True)


def gathered_once(x, axis):
    leaves = jax.tree.leaves(x)
    order = sorted(range(len(leaves)), key=lambda k: -leaves[k].size)
    width = (1, *leaves[order[0]].shape)[-1]
    lines = [
        jnp.pad(leaves[k].reshape(-1), (0, -leaves[k].size % width)).reshape(-1, width)
        for k in order
    ]
    both, at, found = (copy_for_each(jnp.concatenate(lines), axis), 0, {})
    for k, line in zip(order, lines):
        section = both[:, at : at + len(line)].reshape(len(both), -1)
        found[k] = section[:, : leaves[k].size].reshape(-1, *leaves[k].shape)
        at += len(line)
    numbers = iter(range(len(leaves)))
    return jax.tree.map(lambda _: found[next(numbers)], x)


def combined_pairwise(pieces, combine):
    while len(jax.tree.leaves(pieces)[0]) > 1:
        pieces = jax.vmap(combine)(
            *(jax.tree.map(lambda part: part[side::2], pieces) for side in (0, 1))
        )
    return jax.tree.map(lambda part: part[0], pieces)


def entering(x, axis, combine, identity):
    peers, mine = (lax.axis_size(axis), lax.axis_index(axis))
    passed = jnp.arange(peers) < mine

    def kept(part, zero, own):
        part = jnp.where(
            passed.reshape(-1, *(1 for _ in own.shape)), part, jnp.asarray(zero, own.dtype)
        )
        return part

    pieces = gathered_once(x, axis)
    return combined_pairwise(jax.tree.map(kept, pieces, identity, x), combine)


def shifted(x, axis, by):
    peers = lax.axis_size(axis)
    pairs = [(i, i + by) for i in range(peers) if 0 <= i + by < peers]
    return lax.ppermute(x, axis, pairs)


def split_up(x, dim, peers):
    shape = x.shape
    blocks = x.reshape(*shape[:dim], peers, shape[dim] // peers, *shape[dim + 1 :])
    return jnp.moveaxis(blocks, dim, 0)


def summed_on_arrival(x, axis, dim):
    blocks = split_up(x, dim, lax.axis_size(axis))
    arrived = lax.all_to_all(blocks, axis, split_axis=0, concat_axis=0, tiled=True)
    return arrived.sum(axis=0)


def join_bounds(earlier, later):
    early_first, early_last, early_start = earlier
    late_first, late_last, late_start = later
    first_id = jnp.where(early_first < 0, late_first, early_first)
    carried = (late_first == late_last) & (early_last == late_last)
    start_pos = jnp.where(late_last < 0, early_start, jnp.where(carried, early_start, late_start))
    last_id = jnp.where(late_last < 0, early_last, late_last)
    return (first_id, last_id, start_pos)


def on_device(features, queries, out_grad, doc_ids, key_weight):
    tokens = features[0]
    tok_count = tokens.shape[0]
    group_size = HQ // KVH
    query_rows = queries[0].reshape(tok_count, KVH, group_size, HD)
    grad_rows = out_grad[0].reshape(tok_count, KVH, group_size, HD)
    doc_local = doc_ids[0]
    full_weight = gather_axes(key_weight, SECTION, (0, 1), 0)
    key_sum = jnp.dot(tokens, full_weight, preferred_element_type=jnp.float32)
    keys_local = key_sum.astype(jnp.bfloat16)
    offset = lax.axis_index(SEQ) * tok_count
    smaller = (doc_local[None, :] < doc_local[:, None]).astype(jnp.int32)
    local_first = offset + jnp.sum(smaller, axis=1)
    summary = (doc_local[0], doc_local[-1], local_first[-1])
    missing = jnp.int32(-1)
    prefix = entering(summary, SEQ, join_bounds, (missing, missing, jnp.int32(0)))
    continued = (doc_local == doc_local[0]) & (prefix[1] == doc_local[0])
    doc_start = jnp.where(continued, prefix[2], local_first)
    key_blocks = [keys_local]
    for hop_count in range(1, REACH + 1):
        key_blocks.insert(0, shifted(keys_local, SEQ, hop_count))
    window = jnp.concatenate(key_blocks, axis=0)
    window_len = window.shape[0]
    key_pos = offset - REACH * tok_count + jnp.arange(window_len, dtype=jnp.int32)
    query_pos = offset + jnp.arange(tok_count, dtype=jnp.int32)
    visible = (key_pos[None, :] >= doc_start[:, None]) & (key_pos[None, :] <= query_pos[:, None])
    mask_full = visible[:, None, :]
    score_scale = 1.0 / math.sqrt(HD)
    window_heads = window.reshape(window_len, KVH, HD)
    grad_parts = []
    for head_index in range(KVH):
        scores = (
            jnp.einsum(
                "trd,wd->trw",
                query_rows[:, head_index],
                window_heads[:, head_index],
                preferred_element_type=jnp.float32,
            )
            * score_scale
        )
        masked = jnp.where(mask_full, scores, -1e30)
        row_top = jnp.max(masked, axis=2, keepdims=True)
        weights_exp = jnp.where(mask_full, jnp.exp(masked - row_top), 0.0)
        prob_rows = (weights_exp / jnp.sum(weights_exp, axis=2, keepdims=True)).astype(jnp.bfloat16)
        grad_parts.append(
            jnp.einsum(
                "trw,trd->wd",
                prob_rows,
                grad_rows[:, head_index],
                preferred_element_type=jnp.float32,
            )
        )
    window_grad = jnp.concatenate(grad_parts, axis=1)
    slots = [
        window_grad[index_slot * tok_count : (index_slot + 1) * tok_count]
        for index_slot in range(REACH + 1)
    ]
    own_grad = slots[REACH]
    for hop_count in range(1, REACH + 1):
        own_grad = own_grad + shifted(slots[REACH - hop_count], SEQ, -hop_count)
    value_grad = own_grad.astype(jnp.bfloat16)
    columns = lax.all_to_all(tokens, SEQ, split_axis=1, concat_axis=0, tiled=True)
    grad_block = jnp.einsum(
        "td,tk->dk",
        columns,
        gather_axes(value_grad, SEQ, (0, 1, 2), 0),
        preferred_element_type=jnp.float32,
    )
    return summed_on_arrival(grad_block, SECTION, 1)


def solution(mesh):
    finer = Mesh(
        mesh.devices.reshape(4, 4, 2, 8, 2), ("section_0", "section_1", "seq_0", "seq_1", "seq_2")
    )
    return jax.shard_map(
        on_device,
        mesh=finer,
        in_specs=(
            P(SECTION, SEQ, None),
            P(SECTION, SEQ, None),
            P(SECTION, SEQ, None),
            P(SECTION, SEQ),
            P(SECTION, None),
        ),
        out_specs=P(SEQ, SECTION),
        check_vma=False,
    )
```

profile of v0, /device:TPU:8, one launch (start us, length us, event | category | flops | bytes accessed | tf_op | source)
XLA Modules:
  0.0 341.7 jit_solution(2097719810445383646)
XLA Ops:
  6.5 0.7 all-gather.10.cloned.1.call-update
  7.3 43.4 %all-gather.10.cloned.1.call-done = bf16[1024,512]{1,0:T(8,128)(2,1)} async-done(((bf16[256,512]{1,0:T(8,128)(2,1)}), bf16[1024,512]{1,0:T(8,128)(2,1)}) %all-gather.10.cloned.1.call-update) | async-done | bytes 1048592 | tf_op jit(solution)/shard_map/all_gather | solution.py:26
  50.7 0.9 convert_reduce_fusion
  52.2 1.3 fusion.60
  53.5 2.0 add_bitcast_fusion
  55.5 0.6 broadcast_in_dim.70
  56.1 10.4 %all-to-all-start = ((s32[32,3,1]{1,2,0:T(1,128)}), s32[32,3,1]{1,2,0:T(1,128)S(1)}, u32[]{:S(2)}, u32[]{:S(2)}) async-start(s32[32,3,1]{1,2,0:T(1,128)} %broadcast_in_dim.70), calls=%async_computation | async-start | bytes 32768 | tf_op jit(solution)/shard_map/all_to_all | solution.py:39
  66.6 2.3 copy.115
  68.9 0.7 copy.117
  69.6 8.0 %all-to-all-done = s32[32,3,1]{1,2,0:T(1,128)S(1)} async-done(((s32[32,3,1]{1,2,0:T(1,128)}), s32[32,3,1]{1,2,0:T(1,128)S(1)}, u32[]{:S(2)}, u32[]{:S(2)}) %all-to-all-start) | async-done | bytes 416 | tf_op jit(solution)/shard_map/all_to_all | solution.py:39
  77.6 1.9 slice_reduce_fusion
  81.9 0.6 slice.198
  82.5 0.6 fusion.59
  90.7 0.6 and_select_fusion.4
  91.3 13.7 %all-gather.12.cloned.1.call-done = bf16[16,256,512]{2,1,0:T(8,128)(2,1)} async-done(((bf16[4,256,512]{2,1,0:T(8,128)(2,1)}), bf16[16,256,512]{2,1,0:T(8,128)(2,1)}) %all-gather.12.cloned.1.call-update) | async-done | bytes 4194320 | tf_op jit(solution)/shard_map/all_gather | solution.py:26
  105.1 2.7 copy.113
  107.8 0.7 convolution_convert_fusion
  108.5 4.3 %collective-permute-start = (bf16[128,512]{1,0:T(8,128)(2,1)S(1)}, bf16[128,512]{1,0:T(8,128)(2,1)S(1)}, u32[]{:S(2)}, u32[]{:S(2)}) collective-permute-start(bf16[128,512]{1,0:T(8,128)(2,1)S(1)} %convolution_convert_fusion), channel_id=1, source_target_pairs={{0,4},{1,5},{2,6},{3,7},{4,8},{5,9},{6,10},{7,11},{8,12},{9,13},{1... | collective-permute-start | bytes 393224 | tf_op jit(solution)/shard_map/ppermute | solution.py:84
  112.8 3.6 %collective-permute-start.1 = (bf16[128,512]{1,0:T(8,128)(2,1)S(1)}, bf16[128,512]{1,0:T(8,128)(2,1)S(1)}, u32[]{:S(2)}, u32[]{:S(2)}) collective-permute-start(bf16[128,512]{1,0:T(8,128)(2,1)S(1)} %convolution_convert_fusion), channel_id=1, source_target_pairs={{0,3},{1,4},{2,5},{3,6},{4,7},{5,8},{6,9},{7,10},{8,11},{9,12},{10... | collective-permute-start | bytes 393224 | tf_op jit(solution)/shard_map/ppermute | solution.py:84
  116.6 2.9 collective-permute-start.2
  119.5 2.5 collective-permute-start.3
  122.5 3.8 %collective-permute-done.2 = bf16[128,512]{1,0:T(8,128)(2,1)S(1)} collective-permute-done((bf16[128,512]{1,0:T(8,128)(2,1)S(1)}, bf16[128,512]{1,0:T(8,128)(2,1)S(1)}, u32[]{:S(2)}, u32[]{:S(2)}) %collective-permute-start.2) | collective-permute-done | bytes 131104 | tf_op jit(solution)/shard_map/ppermute | solution.py:84
  126.3 3.3 collective-permute-done.3
  129.9 1.9 fusion.57
  131.8 4.3 %fusion.64 = (f32[128,8]{0,1:T(8,128)}, f32[128,8,640]{0,2,1:T(8,128)}) fusion(pred[128,640]{0,1:T(8,128)(4,1)S(1)} %compare_and_fusion, bf16[128,4,8,128]{0,3,2,1:T(8,128)(2,1)} %bitcast.170, bf16[640,1,128]{2,1,0:T(2,128)(2,1)} %get-tuple-element.12), kind=kOutput, calls=%fused_computation.119 | convolution fusion | flops 171049600 | bytes 3379200 | tf_op jit(solution)/shard_map/sub | solution.py:151
  136.1 4.2 %fusion.63 = (f32[128,8]{0,1:T(8,128)}, f32[128,8,640]{0,2,1:T(8,128)}) fusion(pred[128,640]{0,1:T(8,128)(4,1)S(1)} %compare_and_fusion, bf16[128,4,8,128]{0,3,2,1:T(8,128)(2,1)S(1)} %bitcast.171, bf16[640,1,128]{2,1,0:T(2,128)(2,1)} %get-tuple-element.14), kind=kOutput, calls=%fused_computation.118 | convolution fusion | flops 171049600 | bytes 3215360 | tf_op jit(solution)/shard_map/sub | solution.py:151
  140.3 4.1 %fusion.62 = (f32[128,8]{0,1:T(8,128)}, f32[128,8,640]{0,2,1:T(8,128)}) fusion(pred[128,640]{0,1:T(8,128)(4,1)S(1)} %compare_and_fusion, bf16[128,4,8,128]{0,3,2,1:T(8,128)(2,1)S(1)} %bitcast.172, bf16[640,1,128]{2,1,0:T(2,128)(2,1)} %get-tuple-element.13), kind=kOutput, calls=%fused_computation.117 | convolution fusion | flops 171049600 | bytes 3215360 | tf_op jit(solution)/shard_map/sub | solution.py:151
  144.4 3.2 fusion.61
  147.6 2.4 fusion.27
  150.7 1.2 copy-done.5
  152.5 1.2 copy-done.6
  154.4 1.9 collective-permute-start.4
  156.3 1.9 collective-permute-start.5
  158.2 1.3 collective-permute-start.6
  159.5 1.3 collective-permute-start.7
  161.2 6.1 %collective-permute-done.5 = f32[128,512]{0,1:T(8,128)S(1)} collective-permute-done((f32[128,512]{0,1:T(8,128)S(1)}, f32[128,512]{0,1:T(8,128)S(1)}, u32[]{:S(2)}, u32[]{:S(2)}) %collective-permute-start.5) | collective-permute-done | bytes 262176 | tf_op jit(solution)/shard_map/ppermute | solution.py:84
  167.4 7.1 %collective-permute-done.6 = f32[128,512]{0,1:T(8,128)S(1)} collective-permute-done((f32[128,512]{0,1:T(8,128)S(1)}, f32[128,512]{0,1:T(8,128)S(1)}, u32[]{:S(2)}, u32[]{:S(2)}) %collective-permute-start.6) | collective-permute-done | bytes 262176 | tf_op jit(solution)/shard_map/ppermute | solution.py:84
  174.5 6.6 %collective-permute-done.7 = f32[128,512]{0,1:T(8,128)S(1)} collective-permute-done((f32[128,512]{0,1:T(8,128)S(1)}, f32[128,512]{0,1:T(8,128)S(1)}, u32[]{:S(2)}, u32[]{:S(2)}) %collective-permute-start.7) | collective-permute-done | bytes 262176 | tf_op jit(solution)/shard_map/ppermute | solution.py:84
  181.3 27.6 %all-gather.2 = bf16[256,512]{0,1:T(8,128)(2,1)S(1)} all-gather(bf16[128,512]{0,1:T(8,128)(2,1)S(1)} %fusion.40), channel_id=4, replica_groups=mesh['section_0'=4,'section_1'=4,'seq_0'=2,'seq_1'=8,'seq_2'=2] {'seq_0'}, dimensions={0}, use_global_device_ids=true | all-gather | bytes 393216 | tf_op jit(solution)/shard_map/all_gather | solution.py:26
  208.9 0.8 copy.136
  209.8 61.4 %all-gather.14.cloned.1.call-done = bf16[16,128,512]{2,1,0:T(8,128)(2,1)} async-done(((bf16[2,128,512]{2,1,0:T(8,128)(2,1)}), bf16[16,128,512]{2,1,0:T(8,128)(2,1)}) %all-gather.14.cloned.1.call-update) | async-done | bytes 2097168 | tf_op jit(solution)/shard_map/all_gather | solution.py:26
  271.3 0.7 copy.130
  271.9 43.2 %all_to_all.29 = bf16[128,32,128]{0,2,1:T(8,128)(2,1)S(1)} all-to-all(bf16[128,32,128]{0,2,1:T(8,128)(2,1)S(1)} %bitcast.163), channel_id=1, replica_groups=mesh['section_0'=4,'section_1'=4,'seq_0'=2,'seq_1'=8,'seq_2'=2] {'seq_0'..., dimensions={1} | all-to-all | bytes 2097152 | tf_op jit(solution)/shard_map/all_to_all | solution.py:170
  315.2 0.7 copy.131
  315.9 2.6 copy.129
  318.5 1.3 fusion.65
  319.8 14.7 %all_to_all.30 = f32[16,128,32]{1,2,0:T(8,128)S(1)} all-to-all(f32[16,128,32]{1,2,0:T(8,128)S(1)} %bitcast.176), channel_id=1, replica_groups=mesh['section_0'=4,'section_1'=4,'seq_0'=2,'seq_1'=8,'seq_2'=2] {'sectio..., dimensions={0} | all-to-all | bytes 524288 | tf_op jit(solution)/shard_map/all_to_all | solution.py:95
  334.5 0.6 reduce_sum.59
  (77 shorter events, 7.0 us)
Async XLA Ops:
  6.5 62.4 %copy-start.1 = (bf16[1,128,4096]{2,1,0:T(8,128)(2,1)S(1)}, bf16[1,128,4096]{2,1,0:T(8,128)(2,1)}, u32[]{:S(2)}) copy-start(bf16[1,128,4096]{2,1,0:T(8,128)(2,1)} %param.7) | copy-start | bytes 3145732
  6.5 44.1 %all-gather.10.cloned.1.call-start = ((), (), s32[]{:S(2)}) async-start(), calls=%async_computation.3 | async-start | bytes 1310720 | tf_op jit(solution)/shard_map/all_gather | solution.py:26
  7.3 97.8 %all-gather.12.cloned.1.call-start = ((), (), s32[]{:S(2)}) async-start(), calls=%async_computation.4 | async-start | bytes 5242880 | tf_op jit(solution)/shard_map/all_gather | solution.py:26
  50.7 40.0 %copy-start.3 = (s32[1,128]{1,0:T(1,128)S(1)}, s32[1,128]{1,0:T(1,128)}, u32[]{:S(2)}) copy-start(s32[1,128]{1,0:T(1,128)} %param.8) | copy-start | bytes 1540
  56.1 21.5 %all-to-all-start = ((s32[32,3,1]{1,2,0:T(1,128)}), s32[32,3,1]{1,2,0:T(1,128)S(1)}, u32[]{:S(2)}, u32[]{:S(2)}) async-start(s32[32,3,1]{1,2,0:T(1,128)} %broadcast_in_dim.70), calls=%async_computation | async-start | bytes 32768 | tf_op jit(solution)/shard_map/all_to_all | solution.py:39
  66.5 204.7 %all-gather.14.cloned.1.call-start = ((), (), s32[]{:S(2)}) async-start(), calls=%async_computation.5 | async-start | bytes 2359296 | tf_op jit(solution)/shard_map/all_gather | solution.py:26
  105.1 2.7 copy-start
  108.5 13.6 %collective-permute-start = (bf16[128,512]{1,0:T(8,128)(2,1)S(1)}, bf16[128,512]{1,0:T(8,128)(2,1)S(1)}, u32[]{:S(2)}, u32[]{:S(2)}) collective-permute-start(bf16[128,512]{1,0:T(8,128)(2,1)S(1)} %convolution_convert_fusion), channel_id=1, source_target_pairs={{0,4},{1,5},{2,6},{3,7},{4,8},{5,9},{6,10},{7,11},{8,12},{9,13},{1... | collective-permute-start | bytes 393224 | tf_op jit(solution)/shard_map/ppermute | solution.py:84
  112.8 9.7 %collective-permute-start.1 = (bf16[128,512]{1,0:T(8,128)(2,1)S(1)}, bf16[128,512]{1,0:T(8,128)(2,1)S(1)}, u32[]{:S(2)}, u32[]{:S(2)}) collective-permute-start(bf16[128,512]{1,0:T(8,128)(2,1)S(1)} %convolution_convert_fusion), channel_id=1, source_target_pairs={{0,3},{1,4},{2,5},{3,6},{4,7},{5,8},{6,9},{7,10},{8,11},{9,12},{10... | collective-permute-start | bytes 393224 | tf_op jit(solution)/shard_map/ppermute | solution.py:84
  116.6 9.7 %collective-permute-start.2 = (bf16[128,512]{1,0:T(8,128)(2,1)S(1)}, bf16[128,512]{1,0:T(8,128)(2,1)S(1)}, u32[]{:S(2)}, u32[]{:S(2)}) collective-permute-start(bf16[128,512]{1,0:T(8,128)(2,1)S(1)} %convolution_convert_fusion), channel_id=1, source_target_pairs={{0,2},{1,3},{2,4},{3,5},{4,6},{5,7},{6,8},{7,9},{8,10},{9,11},{10,... | collective-permute-start | bytes 393224 | tf_op jit(solution)/shard_map/ppermute | solution.py:84
  119.5 10.1 %collective-permute-start.3 = (bf16[128,512]{1,0:T(8,128)(2,1)S(1)}, bf16[128,512]{1,0:T(8,128)(2,1)S(1)}, u32[]{:S(2)}, u32[]{:S(2)}) collective-permute-start(bf16[128,512]{1,0:T(8,128)(2,1)S(1)} %convolution_convert_fusion), channel_id=1, source_target_pairs={{0,1},{1,2},{2,3},{3,4},{4,5},{5,6},{6,7},{7,8},{8,9},{9,10},{10,1... | collective-permute-start | bytes 393224 | tf_op jit(solution)/shard_map/ppermute | solution.py:84
  131.8 4.3 %copy-start.2 = (bf16[1,128,4096]{1,2,0:T(8,128)(2,1)S(1)}, bf16[1,128,4096]{1,2,0:T(8,128)(2,1)}, u32[]{:S(2)}) copy-start(bf16[1,128,4096]{1,2,0:T(8,128)(2,1)} %copy.115) | copy-start | bytes 3145732
  147.6 2.5 copy-start.4
  147.6 2.5 copy-start.7
  150.2 1.7 copy-start.5
  150.2 1.7 copy-start.8
  151.9 1.7 copy-start.6
  151.9 1.7 copy-start.9
  154.4 6.9 %collective-permute-start.4 = (f32[128,512]{0,1:T(8,128)S(1)}, f32[128,512]{0,1:T(8,128)S(1)}, u32[]{:S(2)}, u32[]{:S(2)}) collective-permute-start(f32[128,512]{0,1:T(8,128)S(1)} %get-tuple-element.8), channel_id=1, source_target_pairs={{1,0},{2,1},{3,2},{4,3},{5,4},{6,5},{7,6},{8,7},{9,8},{10,9},{11,1... | collective-permute-start | bytes 786440 | tf_op jit(solution)/shard_map/ppermute | solution.py:84
  156.3 11.1 %collective-permute-start.5 = (f32[128,512]{0,1:T(8,128)S(1)}, f32[128,512]{0,1:T(8,128)S(1)}, u32[]{:S(2)}, u32[]{:S(2)}) collective-permute-start(f32[128,512]{0,1:T(8,128)S(1)} %get-tuple-element.11), channel_id=1, source_target_pairs={{2,0},{3,1},{4,2},{5,3},{6,4},{7,5},{8,6},{9,7},{10,8},{11,9},{12,... | collective-permute-start | bytes 786440 | tf_op jit(solution)/shard_map/ppermute | solution.py:84
  158.2 16.3 %collective-permute-start.6 = (f32[128,512]{0,1:T(8,128)S(1)}, f32[128,512]{0,1:T(8,128)S(1)}, u32[]{:S(2)}, u32[]{:S(2)}) collective-permute-start(f32[128,512]{0,1:T(8,128)S(1)} %get-tuple-element.10), channel_id=1, source_target_pairs={{3,0},{4,1},{5,2},{6,3},{7,4},{8,5},{9,6},{10,7},{11,8},{12,9},{13... | collective-permute-start | bytes 786440 | tf_op jit(solution)/shard_map/ppermute | solution.py:84
  159.5 21.6 %collective-permute-start.7 = (f32[128,512]{0,1:T(8,128)S(1)}, f32[128,512]{0,1:T(8,128)S(1)}, u32[]{:S(2)}, u32[]{:S(2)}) collective-permute-start(f32[128,512]{0,1:T(8,128)S(1)} %get-tuple-element.9), channel_id=1, source_target_pairs={{4,0},{5,1},{6,2},{7,3},{8,4},{9,5},{10,6},{11,7},{12,8},{13,9},{1... | collective-permute-start | bytes 786440 | tf_op jit(solution)/shard_map/ppermute | solution.py:84
  209.8 106.1 %all-gather.16.cloned.1.call-start = ((), (), s32[]{:S(2)}) async-start(), calls=%async_computation.6 | async-start | bytes 6291456 | tf_op jit(solution)/shard_map/all_gather | solution.py:26
Sparse Core Ops, SparseCore 0:
  9.4 41.1 all-gather.9
  52.8 52.2 all-gather.11
  209.9 61.3 all-gather.13
  273.2 20.7 all-gather.15
where the time goes:
time: 342 us
  waiting for transfers between devices  155 us (45%)
  blocking collectives  85.6 us (25%)
  starting transfers between devices  30.3 us (9%)
  local copies, waits for them, and re-layouts  23.7 us (7%)
  matrix products  21.9 us (6%)
  between operations  20.5 us (6%)
  other arithmetic  4.54 us (1%)
    all_gather x4, waiting for transfers between devices, stacked_from(): blocks = lax.all_gather(blocks, axes[k])  119 us
    all_to_all x1, blocking collectives, on_device(): lax.all_to_all(tokens, SEQ, split_axis=1, concat_axis=0, tiled=True)  43.2 us
    ppermute x8, waiting for transfers between devices, shifted(): return lax.ppermute(x, axis, pairs)  27.9 us
    all_gather x1, blocking collectives, stacked_from(): blocks = lax.all_gather(blocks, axes[k])  27.6 us
    ppermute x8, starting transfers between devices, shifted(): return lax.ppermute(x, axis, pairs)  19.8 us
    sub x4, matrix products, on_device(): weights_exp = jnp.where(mask_full, jnp.exp(masked - row_top), 0.0)  15.8 us
    all_to_all x1, blocking collectives, summed_on_arrival(): lax.all_to_all(blocks, axis, split_axis=0, concat_axis=0, tiled=True)  14.7 us
    all_to_all x1, starting transfers between devices, copy_for_each(): return lax.all_to_all(copies, axis, split_axis=0, concat_axis=0, tiled=True)  10.4 us
  transfers between devices with their start and end apart: 13, of which 11 were waited for; matrix products, arithmetic and copies ran while one was open for 5% of the time, Pallas kernels for 0%

commit v1 on v0

v1 whole, which is shorter than its diff:
```python
import functools
import math

import jax
import jax.numpy as jnp
from jax import lax
from jax.experimental import pallas as pl
from jax.experimental.pallas import tpu as pltpu
from jax.sharding import Mesh
from jax.sharding import PartitionSpec as P

HQ = 32
KVH = 4
HD = 128
GROUP = HQ // KVH
REACH = 4
ZL, X, ZH, YQ, YB, C = "zl", "x", "zh", "yq", "yb", "core"
SECTION = (ZL, X)
SEQ = (ZH, YQ, YB, C)
CHIPS = (ZH, YQ, YB)
FAR = -1e30


def cyclic(x, axis, by):
    peers = lax.axis_size(axis)
    return lax.ppermute(x, axis, [(i, (i + by) % peers) for i in range(peers)])


def shifted(x, axis, by):
    peers = lax.axis_size(axis)
    pairs = [(i, i + by) for i in range(peers) if 0 <= i + by < peers]
    return lax.ppermute(x, axis, pairs)


def pick(index, halves):
    return jnp.where(index == 0, halves[0], halves[1])


def attention_kernel(tok, bias_ref, k_refs, q_refs, g_refs, far_ref, near_ref, own_ref):
    heads = k_refs[0].shape[1] // HD
    rate = math.log2(math.e) / math.sqrt(HD)
    bias = bias_ref
    for g in range(heads):
        cols = slice(g * HD, (g + 1) * HD)
        keys = jnp.concatenate([k[:, cols] for k in k_refs], axis=0)
        total = None
        for r in range(GROUP):
            h = g * GROUP + r
            wide = slice(h * HD, (h + 1) * HD)
            q = jnp.concatenate([x[:, wide] for x in q_refs], axis=0)
            grad = jnp.concatenate([x[:, wide] for x in g_refs], axis=0)
            scores = lax.dot_general(
                keys, q, (((1,), (1,)), ((), ())), preferred_element_type=jnp.float32
            )
            scores = scores + bias[...]
            top = jnp.max(scores, axis=0, keepdims=True)
            weight = jnp.exp2((scores - top) * rate)
            inverse = 1.0 / jnp.sum(weight, axis=0, keepdims=True)
            probs = (weight * inverse).astype(jnp.bfloat16)
            term = jnp.dot(probs, grad, preferred_element_type=jnp.float32)
            total = term if total is None else total + term
        far_ref[:, cols] = total[: 2 * tok].astype(far_ref.dtype)
        near_ref[:, cols] = total[2 * tok : 4 * tok].astype(near_ref.dtype)
        own_ref[:, cols] = total[4 * tok :]


def attention(bias, keys, queries, grads):
    tok, width = keys[-1].shape[0], keys[-1].shape[1]

    def kernel(*refs):
        n_k, n_q = len(keys), len(queries)
        bias_ref, refs = refs[0], refs[1:]
        k_refs, refs = refs[:n_k], refs[n_k:]
        q_refs, refs = refs[:n_q], refs[n_q:]
        g_refs, refs = refs[:n_q], refs[n_q:]
        attention_kernel(tok, bias_ref, k_refs, q_refs, g_refs, *refs)

    return pl.pallas_call(
        kernel,
        name="attention",
        out_shape=(
            jax.ShapeDtypeStruct((2 * tok, width), jnp.bfloat16),
            jax.ShapeDtypeStruct((2 * tok, width), jnp.bfloat16),
            jax.ShapeDtypeStruct((2 * tok, width), jnp.float32),
        ),
    )(bias, *keys, *queries, *grads)


def on_device(features, queries, out_grad, doc_ids, key_weight):
    tokens = features[0]
    tok, depth = tokens.shape
    core, x_at = lax.axis_index(C), lax.axis_index(X)
    n_zl, n_x = lax.axis_size(ZL), lax.axis_size(X)
    n_zh, n_yq = lax.axis_size(ZH), lax.axis_size(YQ)
    rows, kv_width = key_weight.shape
    half = kv_width // 2

    by_x = tokens.reshape(tok, n_zl, n_x, rows)

    def block_for(k):
        at = (x_at + k) % n_x
        return lax.dynamic_slice_in_dim(by_x, at, 1, 2).reshape(tok, n_zl * rows)

    parts = [block_for(0)] + [cyclic(block_for(k), X, k) for k in range(1, n_x)]

    mine = pick(core, (key_weight[:, :half], key_weight[:, half:]))
    weight_own = lax.all_gather(mine, ZL, tiled=True)
    weight_oth = cyclic(weight_own, C, 1)

    def partial(part):
        own = jnp.dot(part, weight_own, preferred_element_type=jnp.float32)
        oth = jnp.dot(part, weight_oth, preferred_element_type=jnp.float32)
        return jnp.concatenate([own, oth], axis=1)

    total = partial(parts[0])
    for k in range(1, n_x):
        total = total + cyclic(partial(parts[k]).astype(jnp.bfloat16), X, -k)
    keys = total.astype(jnp.bfloat16)
    keys_chip = jnp.concatenate([keys[:, :half], cyclic(keys[:, half:], C, 1)], axis=0)
    keys_near = shifted(keys_chip, CHIPS, 1)
    keys_far = shifted(keys_chip, CHIPS, 2)

    def both_cores(rows_all):
        wide = rows_all.shape[1] // 2
        first, last = rows_all[:, :wide], rows_all[:, wide:]
        return pick(core, (first, last)), cyclic(pick(core, (last, first)), C, 1)

    q_pair = both_cores(queries[0])
    g_pair = both_cores(out_grad[0])

    docs = doc_ids[0]
    docs_chip = jnp.concatenate([docs, cyclic(docs, C, 1)])
    docs_win = jnp.concatenate(
        [shifted(docs_chip, CHIPS, 2), shifted(docs_chip, CHIPS, 1), docs_chip]
    )
    chip = lax.axis_index(CHIPS)
    step = jnp.arange(tok, dtype=jnp.int32)
    pos_chip = jnp.concatenate([core * tok + step, (1 - core) * tok + step]) + chip * 2 * tok
    pos_win = jnp.concatenate([pos_chip - 4 * tok, pos_chip - 2 * tok, pos_chip])
    visible = (
        (docs_win[:, None] == docs_chip[None, :])
        & (pos_win[:, None] <= pos_chip[None, :])
        & (pos_win[:, None] >= 0)
    )
    bias = jnp.where(visible, 0.0, FAR).astype(jnp.float32)

    far, near, own = attention(bias, (keys_far, keys_near, keys_chip[:tok], keys_chip[tok:]), q_pair, g_pair)
    own = own + shifted(near, CHIPS, -1) + shifted(far, CHIPS, -2)
    value_chip = own.astype(jnp.bfloat16)
    value_all = jnp.concatenate([value_chip, cyclic(value_chip, YB, 1)], axis=0)

    yb_at = lax.axis_index(YB)
    by_yb = tokens.reshape(tok, n_zh * n_yq, 2, depth // (n_zh * n_yq * 2))
    first = by_yb[:, :, 0].reshape(tok, depth // 2)
    last = by_yb[:, :, 1].reshape(tok, depth // 2)
    own_rows = pick(yb_at, (first, last))
    pair_rows = cyclic(pick(yb_at, (last, first)), YB, 1)
    two = jnp.concatenate([own_rows, pair_rows], axis=0)
    four = cyclic(two, C, 1)
    feat_all = jnp.concatenate([two[:tok], four[:tok], two[tok:], four[tok:]], axis=0)

    block = lax.dot_general(
        value_all, feat_all, (((0,), (0,)), ((), ())), preferred_element_type=jnp.float32
    ).astype(jnp.bfloat16)
    n_zb = n_zl // 2
    out_cols = half // (n_zb * n_x)
    block = block.reshape(n_zb, n_x, out_cols, depth // 2).transpose(1, 0, 2, 3)
    arrived = lax.all_to_all(block, X, split_axis=0, concat_axis=0, tiled=True)
    summed = sum(arrived[k].astype(jnp.float32) for k in range(n_x)).astype(jnp.bfloat16)
    by_core = summed.reshape(n_zb, out_cols, n_zh * n_yq, 2, tok)
    keep = pick(core, (by_core[:, :, :, 0], by_core[:, :, :, 1]))
    give = pick(core, (by_core[:, :, :, 1], by_core[:, :, :, 0]))
    came = cyclic(give, C, 1)
    low, high = pick(core, (keep, came)), pick(core, (came, keep))
    last = jnp.concatenate([low, high], axis=0).transpose(0, 2, 1, 3)
    last = last.reshape(n_zl * n_zh * n_yq, out_cols, tok)
    ended = lax.all_to_all(last, (ZL, ZH, YQ), split_axis=0, concat_axis=0, tiled=True)
    return ended.astype(jnp.float32).sum(axis=0).T


def solution(mesh):
    n_section, n_seq = mesh.devices.shape
    sizes = (n_section // 4, 4, 2, n_seq // 8, 2, 2)
    finer = Mesh(mesh.devices.reshape(sizes), (ZL, X, ZH, YQ, YB, C))
    return jax.shard_map(
        on_device,
        mesh=finer,
        in_specs=(
            P(SECTION, SEQ, None),
            P(SECTION, SEQ, None),
            P(SECTION, SEQ, None),
            P(SECTION, SEQ),
            P(SECTION, None),
        ),
        out_specs=P(SEQ, SECTION),
        check_vma=False,
    )
```

time: 342 us -> 183 us (0.54)
  waiting for transfers between devices: 155 us -> 18.6 us
  starting transfers between devices: 30.3 us -> 60.1 us
  between operations: 20.5 us -> 0.66 us
  local copies, waits for them, and re-layouts: 23.7 us -> 4.96 us
  matrix products: 21.9 us -> 8.63 us
  blocking collectives: 85.6 us -> 75.5 us
  Pallas kernels: 0 us -> 7.8 us
    all_gather x4 -> x0, waiting for transfers between devices: 119 us -> none  [stacked_from(): blocks = lax.all_gather(blocks, axes[k])]
    ppermute x0 -> x15, starting transfers between devices: none -> 43.2 us  [cyclic(): return lax.ppermute(x, axis, [(i, (i + by) % peers) for i in range(peers)])]
    sub x4 -> x0, matrix products: 15.8 us -> none  [on_device(): weights_exp = jnp.where(mask_full, jnp.exp(masked - row_top), 0.0)]
    ppermute x8 -> x6, waiting for transfers between devices: 27.9 us -> 13.5 us  [shifted(): return lax.ppermute(x, axis, pairs)]
    all_to_all x1 -> x0, starting transfers between devices: 10.4 us -> none  [copy_for_each(): return lax.all_to_all(copies, axis, split_axis=0, concat_axis=0, tiled=True)]
    slice x32 -> x2, local copies, waits for them, and re-layouts: 9.91 us -> 0.08 us  [the longest x1 0.07 us: on_device(): four[:tok]]
    all_gather x1, blocking collectives: 27.6 us -> 18.1 us  [on_device(): weight_own = lax.all_gather(mine, ZL, tiled=True)]
    all_to_all x1 -> x0, waiting for transfers between devices: 7.98 us -> none  [copy_for_each(): return lax.all_to_all(copies, axis, split_axis=0, concat_axis=0, tiled=True)]
  transfers between devices with their start and end apart: 13 -> 21, of which waited for: 11 -> 7; matrix products, arithmetic and copies ran while one was open for 5% -> 7% of each run, Pallas kernels for 0% -> 4%
where the time goes in v1:
time: 183 us; the launch traced here: 182 us
  blocking collectives  75.5 us (41%)
  starting transfers between devices  60.1 us (33%)
  waiting for transfers between devices  18.6 us (10%)
  matrix products  8.63 us (5%)
  Pallas kernels  7.8 us (4%)
  other arithmetic  6.05 us (3%)
  local copies, waits for them, and re-layouts  4.96 us (3%)
    ppermute x15, starting transfers between devices, cyclic(): return lax.ppermute(x, axis, [(i, (i + by) % peers) for i in range(peers)])  43.2 us
    all_to_all x1, blocking collectives, on_device(): lax.all_to_all(last, (ZL, ZH, YQ), split_axis=0, concat_axis=0, tiled=True)  40.5 us
    all_gather x1, blocking collectives, on_device(): weight_own = lax.all_gather(mine, ZL, tiled=True)  18.1 us
    ppermute x6, starting transfers between devices, shifted(): return lax.ppermute(x, axis, pairs)  16.9 us
    all_to_all x1, blocking collectives, on_device(): arrived = lax.all_to_all(block, X, split_axis=0, concat_axis=0, tiled=True)  16.8 us
    ppermute x6, waiting for transfers between devices, shifted(): return lax.ppermute(x, axis, pairs)  13.5 us
    pallas_call x1, Pallas kernels, attention(): pl.pallas_call(kernel, name='attention', out_shape=(jax.ShapeDtypeStruct(...  7.8 us
    ppermute x15, waiting for transfers between devices, cyclic(): return lax.ppermute(x, axis, [(i, (i + by) % peers) for i in range(peers)])  5.1 us
  transfers between devices with their start and end apart: 21, of which 7 were waited for; matrix products, arithmetic and copies ran while one was open for 7% of the time, Pallas kernels for 4%

profile of v1, /device:TPU:8, one launch (start us, length us, event | category | flops | bytes accessed | tf_op | source)
XLA Modules:
  0.0 182.3 jit_solution(18140263926998592161)
XLA Ops:
  0.0 1.6 copy.15
  1.7 0.9 constant_dynamic-slice_fusion.2
  2.6 3.5 %collective-permute-start.4 = (bf16[128,1024]{0,1:T(8,128)(2,1)}, bf16[128,1024]{0,1:T(8,128)(2,1)}, u32[]{:S(2)}, u32[]{:S(2)}) collective-permute-start(bf16[128,1024]{0,1:T(8,128)(2,1)} %bitcast.3), channel_id=1, source_target_pairs={{0,32},{32,64},{64,96},{96,0},{1,33},{33,65},{65,97},{97,1},{2,34}... | collective-permute-start | bytes 786440 | tf_op jit(solution)/shard_map/ppermute | solution.py:26
  6.2 18.1 %all_gather.3 = bf16[1024,256]{1,0:T(8,128)(2,1)S(1)} all-gather(bf16[256,256]{1,0:T(8,128)(2,1)S(1)} %slice_select_fusion), channel_id=1, replica_groups=mesh['zl'=4,'x'=4,'zh'=2,'yq'=4,'yb'=2,'core'=2] {'zl'}, dimensions={0}, use_global_device_ids=true | all-gather | bytes 655360 | tf_op jit(solution)/shard_map/all_gather | solution.py:107
  24.3 1.9 %collective-permute-start.3 = (bf16[1024,256]{1,0:T(8,128)(2,1)S(1)}, bf16[1024,256]{1,0:T(8,128)(2,1)S(1)}, u32[]{:S(2)}, u32[]{:S(2)}) collective-permute-start(bf16[1024,256]{1,0:T(8,128)(2,1)S(1)} %all_gather.3), channel_id=1, source_target_pairs={{0,1},{1,0},{2,3},{3,2},{4,5},{5,4},{6,7},{7,6},{8,9},{9,8},{10,11... | collective-permute-start | bytes 1572872 | tf_op jit(solution)/shard_map/ppermute | solution.py:26
  26.2 4.6 %collective-permute-start.6 = (bf16[128,1024]{0,1:T(8,128)(2,1)}, bf16[128,1024]{0,1:T(8,128)(2,1)}, u32[]{:S(2)}, u32[]{:S(2)}) collective-permute-start(bf16[128,1024]{0,1:T(8,128)(2,1)} %bitcast.56), channel_id=1, source_target_pairs={{0,64},{32,96},{64,0},{96,32},{1,65},{33,97},{65,1},{97,33},{2,66}... | collective-permute-start | bytes 786440 | tf_op jit(solution)/shard_map/ppermute | solution.py:26
  30.9 3.3 %collective-permute-start.8 = (bf16[128,1024]{0,1:T(8,128)(2,1)}, bf16[128,1024]{0,1:T(8,128)(2,1)}, u32[]{:S(2)}, u32[]{:S(2)}) collective-permute-start(bf16[128,1024]{0,1:T(8,128)(2,1)} %bitcast.55), channel_id=1, source_target_pairs={{0,96},{32,0},{64,32},{96,64},{1,97},{33,1},{65,33},{97,65},{2,98}... | collective-permute-start | bytes 786440 | tf_op jit(solution)/shard_map/ppermute | solution.py:26
  34.2 1.9 %collective-permute-start = (s32[128]{0:T(128)S(1)}, s32[128]{0:T(128)S(1)}, u32[]{:S(2)}, u32[]{:S(2)}) collective-permute-start(s32[128]{0:T(128)S(1)} %bitcast.58), channel_id=1, source_target_pairs={{0,1},{1,0},{2,3},{3,2},{4,5},{5,4},{6,7},{7,6},{8,9},{9,8},{10,11... | collective-permute-start | bytes 1544 | tf_op jit(solution)/shard_map/ppermute | solution.py:26
  36.5 0.9 broadcast_select_fusion.4
  37.9 0.9 broadcast_select_fusion.2
  38.9 2.4 %collective-permute-start.13 = (bf16[128,2048]{1,0:T(8,128)(2,1)S(1)}, bf16[128,2048]{1,0:T(8,128)(2,1)S(1)}, u32[]{:S(2)}, u32[]{:S(2)}) collective-permute-start(bf16[128,2048]{1,0:T(8,128)(2,1)S(1)} %get-tuple-element.15), channel_id=1, source_target_pairs={{0,1},{1,0},{2,3},{3,2},{4,5},{5,4},{6,7},{7,6},{8,9},{9,8},{10,11... | collective-permute-start | bytes 1572872 | tf_op jit(solution)/shard_map/ppermute | solution.py:26
  41.4 1.9 %collective-permute-start.14 = (bf16[128,2048]{1,0:T(8,128)(2,1)S(1)}, bf16[128,2048]{1,0:T(8,128)(2,1)S(1)}, u32[]{:S(2)}, u32[]{:S(2)}) collective-permute-start(bf16[128,2048]{1,0:T(8,128)(2,1)S(1)} %get-tuple-element.13), channel_id=1, source_target_pairs={{0,1},{1,0},{2,3},{3,2},{4,5},{5,4},{6,7},{7,6},{8,9},{9,8},{10,11... | collective-permute-start | bytes 1572872 | tf_op jit(solution)/shard_map/ppermute | solution.py:26
  43.3 1.2 convolution_convert_fusion.6
  44.5 3.4 %collective-permute-start.18 = (bf16[128,2048]{0,1:T(8,128)(2,1)S(1)}, bf16[128,2048]{0,1:T(8,128)(2,1)S(1)}, u32[]{:S(2)}, u32[]{:S(2)}) collective-permute-start(bf16[128,2048]{0,1:T(8,128)(2,1)S(1)} %bitcast.54), channel_id=1, source_target_pairs={{0,2},{2,0},{1,3},{3,1},{4,6},{6,4},{5,7},{7,5},{8,10},{10,8},{9,1... | collective-permute-start | bytes 1572872 | tf_op jit(solution)/shard_map/ppermute | solution.py:26
  47.9 1.2 convolution_convert_fusion.4
  49.2 1.2 convolution_convert_fusion.2
  50.4 1.2 convolution_convert_fusion.5
  51.7 2.2 %collective-permute-start.5 = (bf16[128,512]{1,0:T(8,128)(2,1)S(1)}, bf16[128,512]{1,0:T(8,128)(2,1)S(1)}, u32[]{:S(2)}, u32[]{:S(2)}) collective-permute-start(bf16[128,512]{1,0:T(8,128)(2,1)S(1)} %pad_maximum_fusion.1), channel_id=1, source_target_pairs={{0,96},{32,0},{64,32},{96,64},{1,97},{33,1},{65,33},{97,65},{2,98}... | collective-permute-start | bytes 393224 | tf_op jit(solution)/shard_map/ppermute | solution.py:26
  53.9 1.2 convolution_convert_fusion.3
  55.1 4.5 %collective-permute-start.7 = (bf16[128,512]{1,0:T(8,128)(2,1)S(1)}, bf16[128,512]{1,0:T(8,128)(2,1)S(1)}, u32[]{:S(2)}, u32[]{:S(2)}) collective-permute-start(bf16[128,512]{1,0:T(8,128)(2,1)S(1)} %pad_maximum_fusion.2), channel_id=1, source_target_pairs={{0,64},{32,96},{64,0},{96,32},{1,65},{33,97},{65,1},{97,33},{2,66}... | collective-permute-start | bytes 393224 | tf_op jit(solution)/shard_map/ppermute | solution.py:26
  59.7 1.2 convolution_convert_fusion.1
  60.9 3.1 %collective-permute-start.9 = (bf16[128,512]{1,0:T(8,128)(2,1)S(1)}, bf16[128,512]{1,0:T(8,128)(2,1)S(1)}, u32[]{:S(2)}, u32[]{:S(2)}) collective-permute-start(bf16[128,512]{1,0:T(8,128)(2,1)S(1)} %pad_maximum_fusion.3), channel_id=1, source_target_pairs={{0,32},{32,64},{64,96},{96,0},{1,33},{33,65},{65,97},{97,1},{2,34}... | collective-permute-start | bytes 393224 | tf_op jit(solution)/shard_map/ppermute | solution.py:26
  64.5 3.7 %collective-permute-start.1 = (s32[256]{0:T(256)S(1)}, s32[256]{0:T(256)S(1)}, u32[]{:S(2)}, u32[]{:S(2)}) collective-permute-start(s32[256]{0:T(256)S(1)} %pad_add_fusion.2), channel_id=1, source_target_pairs={{0,4},{2,6},{4,8},{6,10},{8,12},{10,14},{12,16},{14,18},{16,20},{1... | collective-permute-start | bytes 3080 | tf_op jit(solution)/shard_map/ppermute | solution.py:32
  68.2 4.7 %collective-permute-start.2 = (s32[256]{0:T(256)S(1)}, s32[256]{0:T(256)S(1)}, u32[]{:S(2)}, u32[]{:S(2)}) collective-permute-start(s32[256]{0:T(256)S(1)} %pad_add_fusion.2), channel_id=1, source_target_pairs={{0,2},{2,4},{4,6},{6,8},{8,10},{10,12},{12,14},{14,16},{16,18},{18... | collective-permute-start | bytes 3080 | tf_op jit(solution)/shard_map/ppermute | solution.py:32
  72.9 1.9 %collective-permute-start.19 = (bf16[256,2048]{0,1:T(8,128)(2,1)S(1)}, bf16[256,2048]{0,1:T(8,128)(2,1)S(1)}, u32[]{:S(2)}, u32[]{:S(2)}) collective-permute-start(bf16[256,2048]{0,1:T(8,128)(2,1)S(1)} %pad_maximum_fusion), channel_id=1, source_target_pairs={{0,1},{1,0},{2,3},{3,2},{4,5},{5,4},{6,7},{7,6},{8,9},{9,8},{10,11... | collective-permute-start | bytes 3145736 | tf_op jit(solution)/shard_map/ppermute | solution.py:26
  74.9 2.4 %collective-permute-start.10 = (bf16[128,256]{1,0:T(8,128)(2,1)S(1)}, bf16[128,256]{1,0:T(8,128)(2,1)S(1)}, u32[]{:S(2)}, u32[]{:S(2)}) collective-permute-start(bf16[128,256]{1,0:T(8,128)(2,1)S(1)} %get-tuple-element.30), channel_id=1, source_target_pairs={{0,1},{1,0},{2,3},{3,2},{4,5},{5,4},{6,7},{7,6},{8,9},{9,8},{10,11... | collective-permute-start | bytes 196616 | tf_op jit(solution)/shard_map/ppermute | solution.py:26
  77.4 0.9 collective-permute-done.10.refs_4_
  78.2 2.7 %collective-permute-start.11 = (bf16[256,256]{1,0:T(8,128)(2,1)S(1)}, bf16[256,256]{1,0:T(8,128)(2,1)S(1)}, u32[]{:S(2)}, u32[]{:S(2)}) collective-permute-start(bf16[256,256]{1,0:T(8,128)(2,1)S(1)} %pad_maximum_fusion.4), channel_id=1, source_target_pairs={{0,4},{2,6},{4,8},{6,10},{8,12},{10,14},{12,16},{14,18},{16,20},{1... | collective-permute-start | bytes 393224 | tf_op jit(solution)/shard_map/ppermute | solution.py:32
  80.9 2.6 %collective-permute-start.12 = (bf16[256,256]{1,0:T(8,128)(2,1)S(1)}, bf16[256,256]{1,0:T(8,128)(2,1)S(1)}, u32[]{:S(2)}, u32[]{:S(2)}) collective-permute-start(bf16[256,256]{1,0:T(8,128)(2,1)S(1)} %pad_maximum_fusion.4), channel_id=1, source_target_pairs={{0,2},{2,4},{4,6},{6,8},{8,10},{10,12},{12,14},{14,16},{16,18},{18... | collective-permute-start | bytes 393224 | tf_op jit(solution)/shard_map/ppermute | solution.py:32
  83.6 1.5 and_select_fusion.refs_0_
  85.1 0.8 copy-done.4
  85.9 1.7 collective-permute-done.11.refs_1_
  87.6 2.2 %collective-permute-done.12.refs_2_ = bf16[256,256]{1,0:T(8,128)(2,1)S(1)} collective-permute-done((bf16[256,256]{1,0:T(8,128)(2,1)S(1)}, bf16[256,256]{1,0:T(8,128)(2,1)S(1)}, u32[]{:S(2)}, u32[]{:S(2)}) %collective-permute-start.12) | collective-permute-done | bytes 131104 | tf_op jit(solution)/shard_map/ppermute | solution.py:32
  89.8 0.6 copy-done.10
  90.5 7.8 %attention.1 = (bf16[256,256]{1,0:T(8,128)(2,1)}, bf16[256,256]{1,0:T(8,128)(2,1)}, f32[256,256]{1,0:T(8,128)}) custom-call(f32[768,256]{1,0:T(8,128)} %and_select_fusion.refs_0_, bf16[256,256]{1,0:T(8,128)(2,1)} %copy-done.9, bf16[256,256]{1,0:T(8,128)(2,1)} %copy-done.10, bf16[128,256]{1,0:T(8,128)(2,1)} %copy-done.2, bf16[128,256]{1,0:T(8,128)(2,1)} %copy-done.8, ...), custom_call_target="tpu_custom_call" | custom-call | tf_op jit(solution)/shard_map/attention/pallas_call | solution.py:78
  98.3 1.9 %collective-permute-start.15 = (bf16[256,256]{1,0:T(8,128)(2,1)}, bf16[256,256]{1,0:T(8,128)(2,1)S(1)}, u32[]{:S(2)}, u32[]{:S(2)}) collective-permute-start(bf16[256,256]{1,0:T(8,128)(2,1)} %get-tuple-element.9), channel_id=1, source_target_pairs={{2,0},{4,2},{6,4},{8,6},{10,8},{12,10},{14,12},{16,14},{18,16},{20... | collective-permute-start | bytes 393224 | tf_op jit(solution)/shard_map/ppermute | solution.py:32
  100.2 1.3 collective-permute-start.16
  101.5 5.8 %collective-permute-done.15 = bf16[256,256]{1,0:T(8,128)(2,1)S(1)} collective-permute-done((bf16[256,256]{1,0:T(8,128)(2,1)}, bf16[256,256]{1,0:T(8,128)(2,1)S(1)}, u32[]{:S(2)}, u32[]{:S(2)}) %collective-permute-start.15) | collective-permute-done | bytes 131104 | tf_op jit(solution)/shard_map/ppermute | solution.py:32
  107.3 3.8 %collective-permute-done.16 = bf16[256,256]{1,0:T(8,128)(2,1)S(1)} collective-permute-done((bf16[256,256]{1,0:T(8,128)(2,1)}, bf16[256,256]{1,0:T(8,128)(2,1)S(1)}, u32[]{:S(2)}, u32[]{:S(2)}) %collective-permute-start.16) | collective-permute-done | bytes 131104 | tf_op jit(solution)/shard_map/ppermute | solution.py:32
  111.1 1.0 add_convert_fusion.1
  112.1 4.0 %collective-permute-start.17 = (bf16[256,256]{1,0:T(8,128)(2,1)S(1)}, bf16[256,256]{1,0:T(8,128)(2,1)S(1)}, u32[]{:S(2)}, u32[]{:S(2)}) collective-permute-start(bf16[256,256]{1,0:T(8,128)(2,1)S(1)} %add_convert_fusion.1), channel_id=1, source_target_pairs={{0,2},{2,0},{1,3},{3,1},{4,6},{6,4},{5,7},{7,5},{8,10},{10,8},{9,1... | collective-permute-start | bytes 393224 | tf_op jit(solution)/shard_map/ppermute | solution.py:26
  116.2 2.9 %collective-permute-done.17 = bf16[256,256]{1,0:T(8,128)(2,1)S(1)} collective-permute-done((bf16[256,256]{1,0:T(8,128)(2,1)S(1)}, bf16[256,256]{1,0:T(8,128)(2,1)S(1)}, u32[]{:S(2)}, u32[]{:S(2)}) %collective-permute-start.17) | collective-permute-done | bytes 131104 | tf_op jit(solution)/shard_map/ppermute | solution.py:26
  119.1 0.8 convolution_convert_fusion
  120.0 16.8 %all_to_all.10 = bf16[4,2,32,2048]{3,2,1,0:T(8,128)(2,1)S(1)} all-to-all(bf16[4,2,32,2048]{3,2,1,0:T(8,128)(2,1)S(1)} %bitcast.45), channel_id=1, replica_groups=mesh['zl'=4,'x'=4,'zh'=2,'yq'=4,'yb'=2,'core'=2] {'x'}, dimensions={0} | all-to-all | bytes 2097152 | tf_op jit(solution)/shard_map/all_to_all | solution.py:168
  137.8 1.9 %collective-permute-start.20 = (bf16[2,32,8,128]{3,2,1,0:T(8,128)(2,1)S(1)}, bf16[2,32,8,128]{3,2,1,0:T(8,128)(2,1)S(1)}, u32[]{:S(2)}, u32[]{:S(2)}) collective-permute-start(bf16[2,32,8,128]{3,2,1,0:T(8,128)(2,1)S(1)} %bitcast.57), channel_id=1, source_target_pairs={{0,1},{1,0},{2,3},{3,2},{4,5},{5,4},{6,7},{7,6},{8,9},{9,8},{10,11... | collective-permute-start | bytes 393224 | tf_op jit(solution)/shard_map/ppermute | solution.py:26
  139.7 1.3 collective-permute-done.20
  141.1 40.5 %all_to_all.11 = bf16[32,32,128]{2,1,0:T(8,128)(2,1)S(1)} all-to-all(bf16[32,32,128]{2,1,0:T(8,128)(2,1)S(1)} %bitcast.53), channel_id=1, replica_groups=mesh['zl'=4,'x'=4,'zh'=2,'yq'=4,'yb'=2,'core'=2] {'zl','zh','yq'}, dimensions={0} | all-to-all | bytes 524288 | tf_op jit(solution)/shard_map/all_to_all | solution.py:177
  181.6 0.7 convert_reduce_fusion
  (64 shorter events, 2.7 us)
Async XLA Ops:
  1.6 4.5 %copy-start.7 = (bf16[256,512]{1,0:T(8,128)(2,1)S(1)}, bf16[256,512]{1,0:T(8,128)(2,1)}, u32[]{:S(2)}) copy-start(bf16[256,512]{1,0:T(8,128)(2,1)} %param.9) | copy-start | bytes 786436
  2.6 31.6 %copy-start.11 = (s32[1,128]{1,0:T(1,128)S(1)}, s32[1,128]{1,0:T(1,128)}, u32[]{:S(2)}) copy-start(s32[1,128]{1,0:T(1,128)} %param.8) | copy-start | bytes 1540
  2.6 33.9 %copy-start = (bf16[1,128,4096]{2,1,0:T(8,128)(2,1)S(1)}, bf16[1,128,4096]{2,1,0:T(8,128)(2,1)}, u32[]{:S(2)}) copy-start(bf16[1,128,4096]{2,1,0:T(8,128)(2,1)} %param.6) | copy-start | bytes 3145732
  2.6 38.8 %collective-permute-start.4 = (bf16[128,1024]{0,1:T(8,128)(2,1)}, bf16[128,1024]{0,1:T(8,128)(2,1)}, u32[]{:S(2)}, u32[]{:S(2)}) collective-permute-start(bf16[128,1024]{0,1:T(8,128)(2,1)} %bitcast.3), channel_id=1, source_target_pairs={{0,32},{32,64},{64,96},{96,0},{1,33},{33,65},{65,97},{97,1},{2,34}... | collective-permute-start | bytes 786440 | tf_op jit(solution)/shard_map/ppermute | solution.py:26
  24.3 26.1 %collective-permute-start.3 = (bf16[1024,256]{1,0:T(8,128)(2,1)S(1)}, bf16[1024,256]{1,0:T(8,128)(2,1)S(1)}, u32[]{:S(2)}, u32[]{:S(2)}) collective-permute-start(bf16[1024,256]{1,0:T(8,128)(2,1)S(1)} %all_gather.3), channel_id=1, source_target_pairs={{0,1},{1,0},{2,3},{3,2},{4,5},{5,4},{6,7},{7,6},{8,9},{9,8},{10,11... | collective-permute-start | bytes 1572872 | tf_op jit(solution)/shard_map/ppermute | solution.py:26
  26.2 18.3 %collective-permute-start.6 = (bf16[128,1024]{0,1:T(8,128)(2,1)}, bf16[128,1024]{0,1:T(8,128)(2,1)}, u32[]{:S(2)}, u32[]{:S(2)}) collective-permute-start(bf16[128,1024]{0,1:T(8,128)(2,1)} %bitcast.56), channel_id=1, source_target_pairs={{0,64},{32,96},{64,0},{96,32},{1,65},{33,97},{65,1},{97,33},{2,66}... | collective-permute-start | bytes 786440 | tf_op jit(solution)/shard_map/ppermute | solution.py:26
  30.9 18.3 %collective-permute-start.8 = (bf16[128,1024]{0,1:T(8,128)(2,1)}, bf16[128,1024]{0,1:T(8,128)(2,1)}, u32[]{:S(2)}, u32[]{:S(2)}) collective-permute-start(bf16[128,1024]{0,1:T(8,128)(2,1)} %bitcast.55), channel_id=1, source_target_pairs={{0,96},{32,0},{64,32},{96,64},{1,97},{33,1},{65,33},{97,65},{2,98}... | collective-permute-start | bytes 786440 | tf_op jit(solution)/shard_map/ppermute | solution.py:26
  34.2 4.7 %collective-permute-start = (s32[128]{0:T(128)S(1)}, s32[128]{0:T(128)S(1)}, u32[]{:S(2)}, u32[]{:S(2)}) collective-permute-start(s32[128]{0:T(128)S(1)} %bitcast.58), channel_id=1, source_target_pairs={{0,1},{1,0},{2,3},{3,2},{4,5},{5,4},{6,7},{7,6},{8,9},{9,8},{10,11... | collective-permute-start | bytes 1544 | tf_op jit(solution)/shard_map/ppermute | solution.py:26
  36.5 1.4 copy-start.1
  38.9 46.2 %collective-permute-start.13 = (bf16[128,2048]{1,0:T(8,128)(2,1)S(1)}, bf16[128,2048]{1,0:T(8,128)(2,1)S(1)}, u32[]{:S(2)}, u32[]{:S(2)}) collective-permute-start(bf16[128,2048]{1,0:T(8,128)(2,1)S(1)} %get-tuple-element.15), channel_id=1, source_target_pairs={{0,1},{1,0},{2,3},{3,2},{4,5},{5,4},{6,7},{7,6},{8,9},{9,8},{10,11... | collective-permute-start | bytes 1572872 | tf_op jit(solution)/shard_map/ppermute | solution.py:26
  41.4 43.7 %collective-permute-start.14 = (bf16[128,2048]{1,0:T(8,128)(2,1)S(1)}, bf16[128,2048]{1,0:T(8,128)(2,1)S(1)}, u32[]{:S(2)}, u32[]{:S(2)}) collective-permute-start(bf16[128,2048]{1,0:T(8,128)(2,1)S(1)} %get-tuple-element.13), channel_id=1, source_target_pairs={{0,1},{1,0},{2,3},{3,2},{4,5},{5,4},{6,7},{7,6},{8,9},{9,8},{10,11... | collective-permute-start | bytes 1572872 | tf_op jit(solution)/shard_map/ppermute | solution.py:26
  44.5 16.4 %collective-permute-start.18 = (bf16[128,2048]{0,1:T(8,128)(2,1)S(1)}, bf16[128,2048]{0,1:T(8,128)(2,1)S(1)}, u32[]{:S(2)}, u32[]{:S(2)}) collective-permute-start(bf16[128,2048]{0,1:T(8,128)(2,1)S(1)} %bitcast.54), channel_id=1, source_target_pairs={{0,2},{2,0},{1,3},{3,1},{4,6},{6,4},{5,7},{7,5},{8,10},{10,8},{9,1... | collective-permute-start | bytes 1572872 | tf_op jit(solution)/shard_map/ppermute | solution.py:26
  51.7 12.8 %collective-permute-start.5 = (bf16[128,512]{1,0:T(8,128)(2,1)S(1)}, bf16[128,512]{1,0:T(8,128)(2,1)S(1)}, u32[]{:S(2)}, u32[]{:S(2)}) collective-permute-start(bf16[128,512]{1,0:T(8,128)(2,1)S(1)} %pad_maximum_fusion.1), channel_id=1, source_target_pairs={{0,96},{32,0},{64,32},{96,64},{1,97},{33,1},{65,33},{97,65},{2,98}... | collective-permute-start | bytes 393224 | tf_op jit(solution)/shard_map/ppermute | solution.py:26
  55.1 13.0 %collective-permute-start.7 = (bf16[128,512]{1,0:T(8,128)(2,1)S(1)}, bf16[128,512]{1,0:T(8,128)(2,1)S(1)}, u32[]{:S(2)}, u32[]{:S(2)}) collective-permute-start(bf16[128,512]{1,0:T(8,128)(2,1)S(1)} %pad_maximum_fusion.2), channel_id=1, source_target_pairs={{0,64},{32,96},{64,0},{96,32},{1,65},{33,97},{65,1},{97,33},{2,66}... | collective-permute-start | bytes 393224 | tf_op jit(solution)/shard_map/ppermute | solution.py:26
  60.9 3.3 %copy-start.5 = (bf16[128,2048]{0,1:T(8,128)(2,1)}, bf16[128,2048]{0,1:T(8,128)(2,1)S(1)}, u32[]{:S(2)}) copy-start(bf16[128,2048]{0,1:T(8,128)(2,1)S(1)} %collective-permute-done.18) | copy-start | bytes 1572868
  60.9 11.9 %collective-permute-start.9 = (bf16[128,512]{1,0:T(8,128)(2,1)S(1)}, bf16[128,512]{1,0:T(8,128)(2,1)S(1)}, u32[]{:S(2)}, u32[]{:S(2)}) collective-permute-start(bf16[128,512]{1,0:T(8,128)(2,1)S(1)} %pad_maximum_fusion.3), channel_id=1, source_target_pairs={{0,32},{32,64},{64,96},{96,0},{1,33},{33,65},{65,97},{97,1},{2,34}... | collective-permute-start | bytes 393224 | tf_op jit(solution)/shard_map/ppermute | solution.py:26
  64.5 10.4 %collective-permute-start.1 = (s32[256]{0:T(256)S(1)}, s32[256]{0:T(256)S(1)}, u32[]{:S(2)}, u32[]{:S(2)}) collective-permute-start(s32[256]{0:T(256)S(1)} %pad_add_fusion.2), channel_id=1, source_target_pairs={{0,4},{2,6},{4,8},{6,10},{8,12},{10,14},{12,16},{14,18},{16,20},{1... | collective-permute-start | bytes 3080 | tf_op jit(solution)/shard_map/ppermute | solution.py:32
  68.2 9.2 %collective-permute-start.2 = (s32[256]{0:T(256)S(1)}, s32[256]{0:T(256)S(1)}, u32[]{:S(2)}, u32[]{:S(2)}) collective-permute-start(s32[256]{0:T(256)S(1)} %pad_add_fusion.2), channel_id=1, source_target_pairs={{0,2},{2,4},{4,6},{6,8},{8,10},{10,12},{12,14},{14,16},{16,18},{18... | collective-permute-start | bytes 3080 | tf_op jit(solution)/shard_map/ppermute | solution.py:32
  72.9 43.3 %collective-permute-start.19 = (bf16[256,2048]{0,1:T(8,128)(2,1)S(1)}, bf16[256,2048]{0,1:T(8,128)(2,1)S(1)}, u32[]{:S(2)}, u32[]{:S(2)}) collective-permute-start(bf16[256,2048]{0,1:T(8,128)(2,1)S(1)} %pad_maximum_fusion), channel_id=1, source_target_pairs={{0,1},{1,0},{2,3},{3,2},{4,5},{5,4},{6,7},{7,6},{8,9},{9,8},{10,11... | collective-permute-start | bytes 3145736 | tf_op jit(solution)/shard_map/ppermute | solution.py:26
  74.9 14.9 %copy-start.2 = (bf16[128,256]{1,0:T(8,128)(2,1)}, bf16[128,256]{1,0:T(8,128)(2,1)S(1)}, u32[]{:S(2)}) copy-start(bf16[128,256]{1,0:T(8,128)(2,1)S(1)} %get-tuple-element.29.refs_3_) | copy-start | bytes 196612
  74.9 3.3 %collective-permute-start.10 = (bf16[128,256]{1,0:T(8,128)(2,1)S(1)}, bf16[128,256]{1,0:T(8,128)(2,1)S(1)}, u32[]{:S(2)}, u32[]{:S(2)}) collective-permute-start(bf16[128,256]{1,0:T(8,128)(2,1)S(1)} %get-tuple-element.30), channel_id=1, source_target_pairs={{0,1},{1,0},{2,3},{3,2},{4,5},{5,4},{6,7},{7,6},{8,9},{9,8},{10,11... | collective-permute-start | bytes 196616 | tf_op jit(solution)/shard_map/ppermute | solution.py:26
  78.2 11.6 %copy-start.8 = (bf16[128,256]{1,0:T(8,128)(2,1)}, bf16[128,256]{1,0:T(8,128)(2,1)S(1)}, u32[]{:S(2)}) copy-start(bf16[128,256]{1,0:T(8,128)(2,1)S(1)} %collective-permute-done.10.refs_4_) | copy-start | bytes 196612
  78.2 9.4 %collective-permute-start.11 = (bf16[256,256]{1,0:T(8,128)(2,1)S(1)}, bf16[256,256]{1,0:T(8,128)(2,1)S(1)}, u32[]{:S(2)}, u32[]{:S(2)}) collective-permute-start(bf16[256,256]{1,0:T(8,128)(2,1)S(1)} %pad_maximum_fusion.4), channel_id=1, source_target_pairs={{0,4},{2,6},{4,8},{6,10},{8,12},{10,14},{12,16},{14,18},{16,20},{1... | collective-permute-start | bytes 393224 | tf_op jit(solution)/shard_map/ppermute | solution.py:32
  80.9 8.9 %collective-permute-start.12 = (bf16[256,256]{1,0:T(8,128)(2,1)S(1)}, bf16[256,256]{1,0:T(8,128)(2,1)S(1)}, u32[]{:S(2)}, u32[]{:S(2)}) collective-permute-start(bf16[256,256]{1,0:T(8,128)(2,1)S(1)} %pad_maximum_fusion.4), channel_id=1, source_target_pairs={{0,2},{2,4},{4,6},{6,8},{8,10},{10,12},{12,14},{14,16},{16,18},{18... | collective-permute-start | bytes 393224 | tf_op jit(solution)/shard_map/ppermute | solution.py:32
  85.1 4.7 %copy-start.3 = (bf16[128,2048]{1,0:T(8,128)(2,1)}, bf16[128,2048]{1,0:T(8,128)(2,1)S(1)}, u32[]{:S(2)}) copy-start(bf16[128,2048]{1,0:T(8,128)(2,1)S(1)} %collective-permute-done.13.refs_6_) | copy-start | bytes 1572868
  85.1 0.8 copy-start.4
  87.6 2.2 %copy-start.9 = (bf16[256,256]{1,0:T(8,128)(2,1)}, bf16[256,256]{1,0:T(8,128)(2,1)S(1)}, u32[]{:S(2)}) copy-start(bf16[256,256]{1,0:T(8,128)(2,1)S(1)} %collective-permute-done.11.refs_1_) | copy-start | bytes 393220
  89.8 0.7 copy-start.10
  98.3 9.0 %collective-permute-start.15 = (bf16[256,256]{1,0:T(8,128)(2,1)}, bf16[256,256]{1,0:T(8,128)(2,1)S(1)}, u32[]{:S(2)}, u32[]{:S(2)}) collective-permute-start(bf16[256,256]{1,0:T(8,128)(2,1)} %get-tuple-element.9), channel_id=1, source_target_pairs={{2,0},{4,2},{6,4},{8,6},{10,8},{12,10},{14,12},{16,14},{18,16},{20... | collective-permute-start | bytes 393224 | tf_op jit(solution)/shard_map/ppermute | solution.py:32
  100.2 10.9 %collective-permute-start.16 = (bf16[256,256]{1,0:T(8,128)(2,1)}, bf16[256,256]{1,0:T(8,128)(2,1)S(1)}, u32[]{:S(2)}, u32[]{:S(2)}) collective-permute-start(bf16[256,256]{1,0:T(8,128)(2,1)} %get-tuple-element.10), channel_id=1, source_target_pairs={{4,0},{6,2},{8,4},{10,6},{12,8},{14,10},{16,12},{18,14},{20,16},{2... | collective-permute-start | bytes 393224 | tf_op jit(solution)/shard_map/ppermute | solution.py:32
  112.1 7.0 %copy-start.6 = (bf16[128,2048]{0,1:T(8,128)(2,1)S(1)}, bf16[128,2048]{0,1:T(8,128)(2,1)}, u32[]{:S(2)}) copy-start(bf16[128,2048]{0,1:T(8,128)(2,1)} %copy-done.5) | copy-start | bytes 1572868
  112.1 7.0 %collective-permute-start.17 = (bf16[256,256]{1,0:T(8,128)(2,1)S(1)}, bf16[256,256]{1,0:T(8,128)(2,1)S(1)}, u32[]{:S(2)}, u32[]{:S(2)}) collective-permute-start(bf16[256,256]{1,0:T(8,128)(2,1)S(1)} %add_convert_fusion.1), channel_id=1, source_target_pairs={{0,2},{2,0},{1,3},{3,1},{4,6},{6,4},{5,7},{7,5},{8,10},{10,8},{9,1... | collective-permute-start | bytes 393224 | tf_op jit(solution)/shard_map/ppermute | solution.py:26
  137.8 3.2 %collective-permute-start.20 = (bf16[2,32,8,128]{3,2,1,0:T(8,128)(2,1)S(1)}, bf16[2,32,8,128]{3,2,1,0:T(8,128)(2,1)S(1)}, u32[]{:S(2)}, u32[]{:S(2)}) collective-permute-start(bf16[2,32,8,128]{3,2,1,0:T(8,128)(2,1)S(1)} %bitcast.57), channel_id=1, source_target_pairs={{0,1},{1,0},{2,3},{3,2},{4,5},{5,4},{6,7},{7,6},{8,9},{9,8},{10,11... | collective-permute-start | bytes 393224 | tf_op jit(solution)/shard_map/ppermute | solution.py:26
